TPU v7x, 256 devices: a whole 4x4x8 slice. The times are simulated.
256 devices in a mesh: seq: 64 (over z, y, core), chan: 4 (over x).
Axes of the slice: x: 4, y: 4, z: 8, core: 2. Of those that a mesh axis runs over, the one named last changes fastest.
Arguments:
- signal: bfloat16 [16384, 2048], P('seq', 'chan'), may hold values from -6 to 6
- gate_rows: bfloat16 [16384, 2048], P('seq', 'chan'), may hold values from -60 to 60
- skip_gain: float32 [2048], P('chan'), may hold values from 0.5 to 1.5
- filter_taps: bfloat16 [16384, 16], P(None, 'chan'), may hold values from -2 to 2
- queries: bfloat16 [16384, 2048], P('seq', 'chan'), may hold values from -6 to 6
- key_rows: bfloat16 [16384, 2048], P('seq', 'chan'), may hold values from -6 to 6
Outputs:
- conv_mixed: bfloat16 [16384, 2048], P('seq', 'chan')
- attended: bfloat16 [256, 1024, 128], P(('chan', 'seq'))
All inputs are finite; a program needn't handle non-finite values.
Results may differ from a plain program's by a relative error of at most 0.0061.
Values may be sent and summed in bfloat16 or wider, within the bound.
A program may use at most 128 MiB of HBM per device.

v0:
```python
import math
import jax
import jax.numpy as jnp
from jax import lax
from jax.sharding import PartitionSpec as P


def toeplitz_block(padded_taps, out_start, in_start, block_rows, group_rows, seq_len):
    heads_loc = padded_taps.shape[0]
    window_len = group_rows + block_rows - 1
    offset = out_start - in_start - block_rows + 1 + seq_len
    window = lax.dynamic_slice_in_dim(padded_taps, offset, window_len, 1)
    flipped = jnp.concatenate(
        [window[:, ::-1], jnp.zeros((heads_loc, 1), padded_taps.dtype)], axis=1
    )
    repeated = jnp.tile(flipped, (1, group_rows))[:, : group_rows * window_len]
    return repeated.reshape(heads_loc, group_rows, window_len)[:, :, group_rows - 1 :]


def add_range(total_acc, inputs, first_row, target, lower, upper, padded_taps, seq_len, head_dim):
    block_rows = inputs.shape[0]
    group_rows = total_acc.shape[0]
    positions = first_row + jnp.arange(block_rows, dtype=jnp.int32)
    keep_rows = (positions >= lower) & (positions < upper)
    is_live = (first_row < upper) & (first_row + block_rows > lower)

    def compute(running):
        masked = jnp.where(keep_rows[:, None], inputs, jnp.zeros_like(inputs))
        matrix = toeplitz_block(padded_taps, target, first_row, block_rows, group_rows, seq_len)
        heads_loc = matrix.shape[0]
        split_in = masked.reshape(block_rows, heads_loc, head_dim)
        product = jnp.einsum("htn,nhd->thd", matrix, split_in, preferred_element_type=jnp.float32)
        return running + product.reshape(group_rows, heads_loc * head_dim)

    def unchanged(running):
        return running

    return lax.cond(is_live, compute, unchanged, total_acc)


def attend_block(q_rows, q_pos, key_end, keys_all, values_all, score_scale):
    key_part = keys_all[:key_end]
    value_part = values_all[:key_end]
    raw_scores = (
        jnp.einsum("qd,kd->qk", q_rows, key_part, preferred_element_type=jnp.float32) * score_scale
    )
    k_pos = jnp.arange(key_end, dtype=jnp.int32)
    masked = jnp.where(k_pos[None, :] <= q_pos[:, None], raw_scores, -jnp.inf)
    peak = jnp.max(masked, axis=1)
    exp_scores = jnp.exp(masked - peak[:, None])
    row_total = jnp.sum(exp_scores, axis=1)
    weighted = jnp.dot(
        exp_scores.astype(jnp.bfloat16), value_part, preferred_element_type=jnp.float32
    )
    return (weighted / row_total[:, None]).astype(jnp.bfloat16)


def shards(signal, gate_rows, skip_gain, filter_taps, queries, key_rows):
    group_rows, local_width = signal.shape
    heads_loc = filter_taps.shape[1]
    head_dim = local_width // heads_loc
    seq_count = lax.axis_size("seq")
    chan_count = lax.axis_size("chan")
    my_group = lax.axis_index("seq")
    seq_len = group_rows * seq_count
    padded_taps = jnp.concatenate(
        [jnp.zeros((seq_len, heads_loc), filter_taps.dtype), filter_taps], axis=0
    ).T
    own_start = my_group * group_rows
    own_upper = own_start + group_rows
    halfway = seq_count // 2
    own_lower = jnp.zeros((), jnp.int32)
    help_upper = jnp.zeros((), jnp.int32)
    help_start = (my_group + halfway) % seq_count * group_rows

    def add_both(totals, inputs, first_row):
        own_acc = add_range(
            totals[0],
            inputs,
            first_row,
            own_start,
            own_lower,
            own_upper,
            padded_taps,
            seq_len,
            head_dim,
        )
        help_acc = add_range(
            totals[1], inputs, first_row, help_start, 0, help_upper, padded_taps, seq_len, head_dim
        )
        return (own_acc, help_acc)

    zero_acc = jnp.zeros((group_rows, local_width), jnp.float32)
    totals = (zero_acc, zero_acc)
    incoming = lax.all_gather(signal, "seq", axis=0, tiled=True)
    incoming_rows = incoming.shape[0]
    pieces_count = incoming_rows // group_rows
    blocks = incoming.reshape(pieces_count, group_rows, local_width)
    starts = group_rows * jnp.arange(pieces_count, dtype=jnp.int32)

    def step_block(running, entry_pair):
        return (add_both(running, entry_pair[0], entry_pair[1]), None)

    totals, unused = lax.scan(step_block, totals, (blocks, starts))
    own_acc, help_acc = totals
    conv_mixed = (
        gate_rows.astype(jnp.float32) * (own_acc + skip_gain[None, :] * signal.astype(jnp.float32))
    ).astype(jnp.bfloat16)
    widened = conv_mixed.astype(jnp.float32)
    squares = jnp.sum(jnp.square(widened), axis=1)
    whole_sum = lax.psum(squares, "chan")
    inv_scale = lax.rsqrt(whole_sum / (local_width * chan_count) + 1e-06)
    values = (widened * inv_scale[:, None]).astype(jnp.bfloat16)
    query_sets = seq_count // heads_loc
    query_rows = group_rows // query_sets
    query_send = (
        queries.reshape(query_sets, query_rows, heads_loc, head_dim)
        .transpose(2, 0, 1, 3)
        .reshape(seq_count, query_rows, head_dim)
    )
    pair_stack = jnp.concatenate(
        [
            key_rows.reshape(group_rows, heads_loc, head_dim),
            values.reshape(group_rows, heads_loc, head_dim),
        ],
        axis=2,
    ).transpose(1, 0, 2)
    pair_send = jnp.broadcast_to(
        pair_stack[:, None], (heads_loc, query_sets, group_rows, 2 * head_dim)
    ).reshape(seq_count, group_rows, 2 * head_dim)
    query_got, pair_got = (
        lax.all_to_all(query_send, "seq", split_axis=0, concat_axis=1, tiled=True),
        lax.all_to_all(pair_send, "seq", split_axis=0, concat_axis=1, tiled=True),
    )
    query_all = query_got[0]
    keys_all = pair_got[0, :, :head_dim]
    values_all = pair_got[0, :, head_dim:]
    my_set = my_group % query_sets
    query_len = query_all.shape[0]
    query_block = min(512, query_len)
    score_scale = 1.0 / math.sqrt(head_dim)
    outputs = []
    for query_step in range(query_len // query_block):
        local_index = query_step * query_block + jnp.arange(query_block, dtype=jnp.int32)
        q_pos = (
            local_index // query_rows * group_rows + my_set * query_rows + local_index % query_rows
        )
        last_source = ((query_step + 1) * query_block - 1) // query_rows
        key_end = (last_source + 1) * group_rows
        q_rows = query_all[query_step * query_block : (query_step + 1) * query_block]
        outputs.append(attend_block(q_rows, q_pos, key_end, keys_all, values_all, score_scale))
    attended = jnp.concatenate(outputs, axis=0)[None]
    return (conv_mixed, attended)


def solution(mesh):
    in_specs = (
        P("seq", "chan"),
        P("seq", "chan"),
        P("chan"),
        P(None, "chan"),
        P("seq", "chan"),
        P("seq", "chan"),
    )
    out_specs = (P("seq", "chan"), P(("chan", "seq"), None, None))
    return jax.shard_map(shards, mesh=mesh, in_specs=in_specs, out_specs=out_specs, check_vma=False)
```

profile of v0, /device:TPU:8, one launch (start us, length us, event | category | flops | bytes accessed | tf_op | source)
XLA Modules:
  0.0 989.2 jit_solution(6087917328609244170)
XLA Ops:
  7.2 0.7 all-gather.2.cloned.1.call-update
  7.9 1.0 reshape.122
  8.9 0.7 copy.16
  9.7 12.1 %all-to-all-start.1 = ((bf16[64,16,128]{2,1,0:T(8,128)(2,1)}), bf16[64,16,128]{2,1,0:T(8,128)(2,1)S(1)}, u32[]{:S(2)}, u32[]{:S(2)}) async-start(bf16[64,16,128]{2,1,0:T(8,128)(2,1)} %bitcast.11), calls=%async_computation.1 | async-start | bytes 524288 | tf_op jit(solution)/shard_map/all_to_all | solution.py:132
  21.8 1.7 reshape.119
  23.5 1.7 pad_bitcast_fusion
  25.2 86.5 %all-gather.2.cloned.1.call-done = bf16[16384,512]{1,0:T(8,128)(2,1)} async-done(((bf16[256,512]{1,0:T(8,128)(2,1)}), bf16[16384,512]{1,0:T(8,128)(2,1)}) %all-gather.2.cloned.1.call-update) | async-done | bytes 16777232 | tf_op jit(solution)/shard_map/all_gather | solution.py:95
  111.7 22.3 %copy.13 = bf16[64,256,512]{1,2,0:T(8,128)(2,1)} copy(bf16[64,256,512]{2,1,0:T(8,128)(2,1)} %bitcast.58) | data formatting | bytes 33554432 | tf_op jit(solution)/shard_map/while | solution.py:104
  134.1 142.4 %while.13 = (s32[]{:T(128)}, f32[256,512]{0,1:T(8,128)S(1)}, s32[64]{0:T(128)S(1)}, s32[]{:T(128)}, bf16[64,256,512]{1,2,0:T(8,128)(2,1)}, /*index=5*/s32[]{:T(1...) while((s32[]{:T(128)}, f32[256,512]{0,1:T(8,128)S(1)}, s32[64]{0:T(128)S(1)}, s32[]{:T(128)}, ...), condition=%wide.region_3.4_spmd, body=%wide.region_0.3_spmd.sunk | while | flops 67372048 | bytes 10779659 | solution.py:104
  135.9 7.0 conditional.2
  137.2 0.8 constant_dynamic-slice_fusion
  138.4 1.0 constant_dynamic-slice_fusion.1
  139.5 0.8 copy.17
  140.7 1.8 reshape.110
  143.0 0.6 dynamic_slice.18
  144.8 7.0 conditional.2
  146.1 0.8 constant_dynamic-slice_fusion
  147.3 1.0 constant_dynamic-slice_fusion.1
  148.4 0.8 copy.17
  149.5 1.8 reshape.110
  153.7 7.0 conditional.2
  154.9 0.8 constant_dynamic-slice_fusion
  156.2 1.0 constant_dynamic-slice_fusion.1
  157.2 0.8 copy.17
  158.4 1.8 reshape.110
  160.7 0.6 dynamic_slice.18
  162.6 0.6 dynamic_slice.18
  166.4 0.6 dynamic_slice.18
  168.3 0.6 dynamic_slice.18
  170.2 0.6 dynamic_slice.18
  174.0 0.6 dynamic_slice.18
  175.9 0.6 dynamic_slice.18
  181.6 0.6 dynamic_slice.18
  183.5 0.6 dynamic_slice.18
  187.3 0.6 dynamic_slice.18
  189.2 0.6 dynamic_slice.18
  191.1 0.6 dynamic_slice.18
  194.9 0.6 dynamic_slice.18
  196.8 0.6 dynamic_slice.18
  198.7 0.6 dynamic_slice.18
  202.5 0.6 dynamic_slice.18
  204.4 0.6 dynamic_slice.18
  206.3 0.6 dynamic_slice.18
  210.0 0.6 dynamic_slice.18
  211.9 0.6 dynamic_slice.18
  217.6 0.6 dynamic_slice.18
  219.5 0.6 dynamic_slice.18
  223.3 0.6 dynamic_slice.18
  225.2 0.6 dynamic_slice.18
  227.1 0.6 dynamic_slice.18
  230.9 0.6 dynamic_slice.18
  276.7 1.2 fusion.28
  277.9 10.4 %psum.7 = f32[256]{0:T(256)S(1)} all-reduce(f32[256]{0:T(256)S(1)} %get-tuple-element.129), channel_id=1, replica_groups=mesh['seq'=64,'chan'=4] {'chan'}, use_global_device_ids=true, to_apply=%region_5.6 | all-reduce | flops 256 | bytes 2048 | tf_op jit(solution)/shard_map/psum | solution.py:111
  288.5 1.2 maximum_bitcast_fusion
  289.8 4.2 broadcast_in_dim.23
  294.0 429.0 %all-to-all-start = ((bf16[64,256,256]{2,1,0:T(8,128)(2,1)}), bf16[64,256,256]{2,1,0:T(8,128)(2,1)}, u32[]{:S(2)}, u32[]{:S(2)}) async-start(bf16[64,256,256]{2,1,0:T(8,128)(2,1)} %bitcast.56), calls=%async_computation | async-start | bytes 16777216 | tf_op jit(solution)/shard_map/all_to_all | solution.py:133
  723.1 186.1 %all-to-all-done = bf16[64,256,256]{2,1,0:T(8,128)(2,1)} async-done(((bf16[64,256,256]{2,1,0:T(8,128)(2,1)}), bf16[64,256,256]{2,1,0:T(8,128)(2,1)}, u32[]{:S(2)}, u32[]{:S(2)}) %all-to-all-start) | async-done | bytes 8388640 | tf_op jit(solution)/shard_map/all_to_all | solution.py:133
  909.2 9.2 fusion.47
  918.4 8.0 fusion.11
  926.4 8.8 fusion.25
  935.2 16.5 %fusion.46 = (f32[512]{0:T(512)S(1)}, f32[512,16384]{0,1:T(8,128)}) fusion(bf16[512,128]{1,0:T(8,128)(2,1)S(1)} %bitcast.61, bf16[1,16384,256]{2,1,0:T(8,128)(2,1)} %bitcast.8, s32[512]{0:T(512)S(1)} %get-tuple-element.138), kind=kOutput, calls=%fused_computation.70 | convolution fusion | flops 2181037568 | bytes 37883904 | tf_op jit(solution)/shard_map/qd,kd->qk/dot_general | solution.py:45
  951.7 15.0 %fusion.6 = f32[512]{0:T(512)S(1)} fusion(f32[512,16384]{0,1:T(8,128)} %get-tuple-element.134, f32[512]{0:T(512)S(1)} %get-tuple-element.133), kind=kLoop, calls=%fused_computation.14 | loop fusion | flops 16776704 | bytes 33558528 | tf_op jit(solution)/shard_map/reduce_sum | solution.py:51
  966.8 14.9 %fusion.19 = bf16[512,128]{1,0:T(8,128)(2,1)S(1)} fusion(bf16[1,16384,256]{2,1,0:T(8,128)(2,1)} %bitcast.8, f32[512,16384]{0,1:T(8,128)} %get-tuple-element.134, f32[512]{0:T(512)S(1)} %get-tuple-element.133, f32[512]{0:T(512)S(1)} %fusion.6), kind=kOutput, calls=%fused_computation.30 | convolution fusion | flops 2164391936 | bytes 37883904 | tf_op jit(solution)/shard_map/dot_general | solution.py:52
  981.7 0.7 maximum_bitcast_fusion.1
  (203 shorter events, 30.5 us)
Async XLA Ops:
  7.2 104.5 %all-gather.2.cloned.1.call-start = ((), (), s32[]{:S(2)}) async-start(), calls=%async_computation.2 | async-start | bytes 17039360 | tf_op jit(solution)/shard_map/all_gather | solution.py:95
  9.7 280.1 %all-to-all-start.1 = ((bf16[64,16,128]{2,1,0:T(8,128)(2,1)}), bf16[64,16,128]{2,1,0:T(8,128)(2,1)S(1)}, u32[]{:S(2)}, u32[]{:S(2)}) async-start(bf16[64,16,128]{2,1,0:T(8,128)(2,1)} %bitcast.11), calls=%async_computation.1 | async-start | bytes 524288 | tf_op jit(solution)/shard_map/all_to_all | solution.py:132
  134.0 142.6 %copy-start = (bf16[256,512]{1,0:T(8,128)(2,1)S(1)}, bf16[256,512]{1,0:T(8,128)(2,1)}, u32[]{:S(2)}) copy-start(bf16[256,512]{1,0:T(8,128)(2,1)} %param.10) | copy-start | bytes 786436
  134.1 142.6 %copy-start.2 = (f32[512]{0:T(512)S(1)}, f32[512]{0:T(512)}, u32[]{:S(2)}) copy-start(f32[512]{0:T(512)} %param.12) | copy-start | bytes 6148
  277.9 640.5 %copy-start.1 = (bf16[256,512]{1,0:T(8,128)(2,1)}, bf16[256,512]{1,0:T(8,128)(2,1)S(1)}, u32[]{:S(2)}) copy-start(bf16[256,512]{1,0:T(8,128)(2,1)S(1)} %get-tuple-element.130) | copy-start | bytes 786436
  294.0 615.1 %all-to-all-start = ((bf16[64,256,256]{2,1,0:T(8,128)(2,1)}), bf16[64,256,256]{2,1,0:T(8,128)(2,1)}, u32[]{:S(2)}, u32[]{:S(2)}) async-start(bf16[64,256,256]{2,1,0:T(8,128)(2,1)} %bitcast.56), calls=%async_computation | async-start | bytes 16777216 | tf_op jit(solution)/shard_map/all_to_all | solution.py:133
Sparse Core Ops, SparseCore 0:
  10.7 100.8 all-gather.1
where the time goes:
time: 997 us; the launch traced here: 989 us
  starting transfers between devices  441 us (44%)
  waiting for transfers between devices  273 us (27%)
  local copies, waits for them, and re-layouts  87.6 us (9%)
  loops' own time  83.6 us (8%)
  matrix products  50.6 us (5%)
  other arithmetic  28.5 us (3%)
  between operations  14.2 us (1%)
  blocking collectives  10.4 us (1%)
    all_to_all x1, starting transfers between devices, shards(): lax.all_to_all(pair_send, 'seq', split_axis=0, concat_axis=1, tiled=True)  429 us
    all_to_all x1, waiting for transfers between devices, shards(): lax.all_to_all(pair_send, 'seq', split_axis=0, concat_axis=1, tiled=True)  186 us
    all_gather x1, waiting for transfers between devices, shards(): incoming = lax.all_gather(signal, 'seq', axis=0, tiled=True)  86.5 us
    another operation x1, loops' own time, shards(): totals, unused = lax.scan(step_block, totals, (blocks, starts))  80.7 us
    dynamic_slice x67, local copies, waits for them, and re-layouts, shards(): totals, unused = lax.scan(step_block, totals, (blocks, starts))  42.6 us
    dot_general x2, matrix products, attend_block(): jnp.einsum('qd,kd->qk', q_rows, key_part, preferred_element_type=jnp.floa...  25.7 us
    dot_general x2, matrix products, attend_block(): jnp.dot(exp_scores.astype(jnp.bfloat16), value_part, preferred_element_ty...  23.7 us
    reduce_sum x2, other arithmetic, attend_block(): row_total = jnp.sum(exp_scores, axis=1)  23.1 us
  transfers between devices with their start and end apart: 3, of which 2 were waited for; matrix products, arithmetic and copies ran while one was open for 9% of the time, Pallas kernels for 0%

commit v1 on v0

--- a/solution.py
+++ b/solution.py
@@ -92,7 +92,9 @@
 
     zero_acc = jnp.zeros((group_rows, local_width), jnp.float32)
     totals = (zero_acc, zero_acc)
-    incoming = lax.all_gather(signal, "seq", axis=0, tiled=True)
+    incoming = jnp.concatenate(
+        lax.all_to_all(jnp.stack([signal] * lax.axis_size("seq")), "seq", 0, 0), axis=0
+    )
     incoming_rows = incoming.shape[0]
     pieces_count = incoming_rows // group_rows
     blocks = incoming.reshape(pieces_count, group_rows, local_width)

time: 997 us -> 1260 us (1.26)
  waiting for transfers between devices: 273 us -> 552 us
  local copies, waits for them, and re-layouts: 87.6 us -> 68.2 us
  starting transfers between devices: 441 us -> 456 us
  between operations: 14.2 us -> 0.82 us
    all_to_all x0 -> x1, waiting for transfers between devices: none -> 366 us  [shards(): lax.all_to_all(jnp.stack([signal] * lax.axis_size('seq')), 'seq', 0, 0)]
    all_gather x1 -> x0, waiting for transfers between devices: 86.5 us -> none  [shards(): incoming = lax.all_gather(signal, 'seq', axis=0, tiled=True)]
    while x2 -> x1, local copies, waits for them, and re-layouts: 22.5 us -> 0.2 us  [shards(): totals, unused = lax.scan(step_block, totals, (blocks, starts))]
  transfers between devices with their start and end apart: 3 -> 3, of which waited for: 2 -> 2; matrix products, arithmetic and copies ran while one was open for 9% -> 5% of each run, Pallas kernels for 0% -> 0%
where the time goes in v1:
time: 1260 us; the launch traced here: 1250 us
  waiting for transfers between devices  552 us (44%)
  starting transfers between devices  456 us (36%)
  loops' own time  85 us (7%)
  local copies, waits for them, and re-layouts  68.2 us (5%)
  matrix products  50.6 us (4%)
  other arithmetic  28.5 us (2%)
    all_to_all x1, starting transfers between devices, shards(): lax.all_to_all(pair_send, 'seq', split_axis=0, concat_axis=1, tiled=True)  432 us
    all_to_all x1, waiting for transfers between devices, shards(): lax.all_to_all(jnp.stack([signal] * lax.axis_size('seq')), 'seq', 0, 0)  366 us
    all_to_all x1, waiting for transfers between devices, shards(): lax.all_to_all(pair_send, 'seq', split_axis=0, concat_axis=1, tiled=True)  186 us
    another operation x1, loops' own time, shards(): totals, unused = lax.scan(step_block, totals, (blocks, starts))  82.1 us
    dynamic_slice x67, local copies, waits for them, and re-layouts, shards(): totals, unused = lax.scan(step_block, totals, (blocks, starts))  41.1 us
    dot_general x2, matrix products, attend_block(): jnp.einsum('qd,kd->qk', q_rows, key_part, preferred_element_type=jnp.floa...  25.7 us
  transfers between devices with their start and end apart: 3, of which 2 were waited for; matrix products, arithmetic and copies ran while one was open for 5% of the time, Pallas kernels for 0%

profile of v1, /device:TPU:8, one launch (start us, length us, event | category | flops | bytes accessed | tf_op | source)
XLA Modules:
  0.0 1252.2 jit_solution(6473332468961747640)
XLA Ops:
  0.6 1.1 copy.14
  1.7 6.1 stack.2
  7.8 12.4 all-to-all-start
  20.3 0.8 copy.17
  21.1 0.8 reshape.117
  21.8 0.8 pad_bitcast_fusion
  22.6 366.4 %all-to-all-done = bf16[64,256,512]{1,2,0:T(8,128)(2,1)} async-done(((bf16[64,256,512]{1,2,0:T(8,128)(2,1)}), bf16[64,256,512]{1,2,0:T(8,128)(2,1)}, u32[]{:S(2)}, u32[]{:S(2)}) %all-to-all-start) | async-done | bytes 16777248 | tf_op jit(solution)/shard_map/all_to_all | solution.py:96
  389.0 11.5 all-to-all-start.2
  400.6 142.4 %while.13 = (s32[]{:T(128)}, f32[256,512]{0,1:T(8,128)S(1)}, s32[64]{0:T(128)S(1)}, s32[]{:T(128)}, bf16[64,256,512]{1,2,0:T(8,128)(2,1)}, /*index=5*/s32[]{:T(1...) while((s32[]{:T(128)}, f32[256,512]{0,1:T(8,128)S(1)}, s32[64]{0:T(128)S(1)}, s32[]{:T(128)}, ...), condition=%wide.region_3.4_spmd, body=%wide.region_0.3_spmd.sunk | while | flops 67372048 | bytes 10779659 | solution.py:106
  400.6 0.6 dynamic_slice.18
  402.5 7.0 conditional.2
  403.1 0.6 compare_and_fusion
  403.7 0.8 constant_dynamic-slice_fusion
  405.0 1.0 constant_dynamic-slice_fusion.1
  406.0 0.8 copy.18
  407.2 1.8 reshape.110
  409.5 0.6 dynamic_slice.18
  411.4 7.0 conditional.2
  412.0 0.6 compare_and_fusion
  412.6 0.8 constant_dynamic-slice_fusion
  413.9 1.0 constant_dynamic-slice_fusion.1
  414.9 0.8 copy.18
  416.1 1.8 reshape.110
  418.4 0.6 dynamic_slice.18
  420.2 7.0 conditional.2
  420.9 0.6 compare_and_fusion
  421.5 0.8 constant_dynamic-slice_fusion
  422.8 1.0 constant_dynamic-slice_fusion.1
  423.8 0.8 copy.18
  425.0 1.8 reshape.110
  427.3 0.6 dynamic_slice.18
  429.2 0.6 dynamic_slice.18
  431.1 0.6 dynamic_slice.18
  433.0 0.6 dynamic_slice.18
  434.9 0.6 dynamic_slice.18
  436.8 0.6 dynamic_slice.18
  438.7 0.6 dynamic_slice.18
  440.6 0.6 dynamic_slice.18
  442.5 0.6 dynamic_slice.18
  444.3 0.6 dynamic_slice.18
  446.2 0.6 dynamic_slice.18
  448.1 0.6 dynamic_slice.18
  450.0 0.6 dynamic_slice.18
  451.9 0.6 dynamic_slice.18
  453.8 0.6 dynamic_slice.18
  455.7 0.6 dynamic_slice.18
  461.4 0.6 dynamic_slice.18
  488.0 0.6 dynamic_slice.18
  497.4 0.6 dynamic_slice.18
  524.0 0.6 dynamic_slice.18
  533.5 0.6 dynamic_slice.18
  543.2 1.2 fusion.28
  544.3 10.5 psum.7
  555.0 1.2 maximum_bitcast_fusion
  556.4 4.2 broadcast_in_dim.23
  560.6 432.2 %all-to-all-start.1 = ((bf16[64,256,256]{2,1,0:T(8,128)(2,1)}), bf16[64,256,256]{2,1,0:T(8,128)(2,1)}, u32[]{:S(2)}, u32[]{:S(2)}) async-start(bf16[64,256,256]{2,1,0:T(8,128)(2,1)} %bitcast.55), calls=%async_computation.1 | async-start | bytes 16777216 | tf_op jit(solution)/shard_map/all_to_all | solution.py:135
  992.8 186.1 %all-to-all-done.1 = bf16[64,256,256]{2,1,0:T(8,128)(2,1)} async-done(((bf16[64,256,256]{2,1,0:T(8,128)(2,1)}), bf16[64,256,256]{2,1,0:T(8,128)(2,1)}, u32[]{:S(2)}, u32[]{:S(2)}) %all-to-all-start.1) | async-done | bytes 8388640 | tf_op jit(solution)/shard_map/all_to_all | solution.py:135
  1178.9 9.2 fusion.47
  1188.1 8.0 fusion.11
  1196.2 8.8 fusion.25
  1205.0 16.5 %fusion.46 = (f32[512]{0:T(512)S(1)}, f32[512,16384]{0,1:T(8,128)}) fusion(bf16[512,128]{1,0:T(8,128)(2,1)S(1)} %bitcast.59, bf16[1,16384,256]{2,1,0:T(8,128)(2,1)} %bitcast.7, s32[512]{0:T(512)S(1)} %get-tuple-element.124), kind=kOutput, calls=%fused_computation.70 | convolution fusion | flops 2181037568 | bytes 37883904 | tf_op jit(solution)/shard_map/qd,kd->qk/dot_general | solution.py:45
  1221.5 15.0 %fusion.6 = f32[512]{0:T(512)S(1)} fusion(f32[512,16384]{0,1:T(8,128)} %get-tuple-element.120, f32[512]{0:T(512)S(1)} %get-tuple-element.119), kind=kLoop, calls=%fused_computation.14 | loop fusion | flops 16776704 | bytes 33558528 | tf_op jit(solution)/shard_map/reduce_sum | solution.py:51
  1236.5 14.9 %fusion.19 = bf16[512,128]{1,0:T(8,128)(2,1)S(1)} fusion(bf16[1,16384,256]{2,1,0:T(8,128)(2,1)} %bitcast.7, f32[512,16384]{0,1:T(8,128)} %get-tuple-element.120, f32[512]{0:T(512)S(1)} %get-tuple-element.119, f32[512]{0:T(512)S(1)} %fusion.6), kind=kOutput, calls=%fused_computation.30 | convolution fusion | flops 2164391936 | bytes 37883904 | tf_op jit(solution)/shard_map/dot_general | solution.py:52
  1251.4 0.7 maximum_bitcast_fusion.1
  (209 shorter events, 29.7 us)
Async XLA Ops:
  7.8 12.4 copy-start.2
  7.8 13.3 %copy-start.3 = (bf16[256,512]{1,0:T(8,128)(2,1)S(1)}, bf16[256,512]{1,0:T(8,128)(2,1)}, u32[]{:S(2)}) copy-start(bf16[256,512]{1,0:T(8,128)(2,1)} %param.15) | copy-start | bytes 786436
  7.8 14.0 %copy-start.4 = (bf16[16384,4]{0,1:T(4,128)(2,1)S(1)}, bf16[16384,4]{0,1:T(4,128)(2,1)}, u32[]{:S(2)}) copy-start(bf16[16384,4]{0,1:T(4,128)(2,1)} %param.13) | copy-start | bytes 393220
  7.8 381.2 %all-to-all-start = ((bf16[64,256,512]{1,2,0:T(8,128)(2,1)}), bf16[64,256,512]{1,2,0:T(8,128)(2,1)}, u32[]{:S(2)}, u32[]{:S(2)}) async-start(bf16[64,256,512]{1,2,0:T(8,128)(2,1)} %stack.2), calls=%async_computation | async-start | bytes 33554432 | tf_op jit(solution)/shard_map/all_to_all | solution.py:96
  389.0 167.3 %all-to-all-start.2 = ((bf16[64,16,128]{2,1,0:T(8,128)(2,1)}), bf16[64,16,128]{2,1,0:T(8,128)(2,1)S(1)}, u32[]{:S(2)}, u32[]{:S(2)}) async-start(bf16[64,16,128]{2,1,0:T(8,128)(2,1)} %bitcast.10), calls=%async_computation.2 | async-start | bytes 524288 | tf_op jit(solution)/shard_map/all_to_all | solution.py:134
  400.6 142.6 %copy-start = (bf16[256,512]{1,0:T(8,128)(2,1)S(1)}, bf16[256,512]{1,0:T(8,128)(2,1)}, u32[]{:S(2)}) copy-start(bf16[256,512]{1,0:T(8,128)(2,1)} %param.10) | copy-start | bytes 786436
  400.6 142.6 %copy-start.5 = (f32[512]{0:T(512)S(1)}, f32[512]{0:T(512)}, u32[]{:S(2)}) copy-start(f32[512]{0:T(512)} %param.12) | copy-start | bytes 6148
  544.3 643.8 %copy-start.1 = (bf16[256,512]{1,0:T(8,128)(2,1)}, bf16[256,512]{1,0:T(8,128)(2,1)S(1)}, u32[]{:S(2)}) copy-start(bf16[256,512]{1,0:T(8,128)(2,1)S(1)} %get-tuple-element.116) | copy-start | bytes 786436
  560.6 618.3 %all-to-all-start.1 = ((bf16[64,256,256]{2,1,0:T(8,128)(2,1)}), bf16[64,256,256]{2,1,0:T(8,128)(2,1)}, u32[]{:S(2)}, u32[]{:S(2)}) async-start(bf16[64,256,256]{2,1,0:T(8,128)(2,1)} %bitcast.55), calls=%async_computation.1 | async-start | bytes 16777216 | tf_op jit(solution)/shard_map/all_to_all | solution.py:135
